TPU v7x, 32 devices: a whole 2x2x4 slice. The times are simulated.
32 devices in a mesh: lon: 8 (over z, y), lat: 4 (over x, core).
Axes of the slice: x: 2, y: 2, z: 4, core: 2. Of those that a mesh axis runs over, the one named last changes fastest.
Arguments:
- crosswise_speed_units: float32 [8, 64, 2048], P(None, 'lat', 'lon'), may hold values from -6 to 6
- poleward_speed_units: float32 [8, 64, 2048], P(None, 'lat', 'lon'), may hold values from -6 to 6
- thermal_anomaly: float32 [8, 64, 2048], P(None, 'lat', 'lon'), may hold values from -6 to 6
- saltiness_anomaly: float32 [8, 64, 2048], P(None, 'lat', 'lon'), may hold values from -6 to 6
- freeboard_elevation: float32 [64, 2048], P('lat', 'lon'), may hold values from -6 to 6
- barotropic_zonal_flow: float32 [64, 2048], P('lat', 'lon'), may hold values from -6 to 6
- barotropic_meridional_flow: float32 [64, 2048], P('lat', 'lon'), may hold values from -6 to 6
- submerged_layer_tally: int32 [64, 2048], P('lat', 'lon'), may hold values from 0 to 8
- seam_partner_index: int32 [2048], P('lon'), may hold values from 0 to 2047, as said below
Outputs:
- zonal_speed_final: float32 [8, 64, 2048], P(None, 'lat', 'lon')
- poleward_speed_final: float32 [8, 64, 2048], P(None, 'lat', 'lon')
- thermal_final: float32 [8, 64, 2048], P(None, 'lat', 'lon')
- saltiness_final: float32 [8, 64, 2048], P(None, 'lat', 'lon')
- freeboard_final: float32 [64, 2048], P('lat', 'lon')
- barotropic_zonal_final: float32 [64, 2048], P('lat', 'lon')
- barotropic_meridional_final: float32 [64, 2048], P('lat', 'lon')
Inputs may be any that keep to these rules, and one draw needn't show every extreme that they name: seam_partner_index[seam_partner_index[c]] = c, and seam_partner_index[(c + 1) mod 2048] = (seam_partner_index[c] - 1) mod 2048 for every column c.
All inputs are finite; a program needn't handle non-finite values.
Results may differ from a plain program's by a relative error of at most 0.0003.
Values sent between devices are 32-bit elements; how exact they have to be, the bound alone decides.
No kernel may reach another device: no remote copies, remote signals or barrier semaphores. Data moves between devices by JAX's collectives and lax.ppermute only.
A program may use at most 128 MiB of HBM per device.

v0:
```python
import jax
import jax.numpy as jnp
from jax import lax
from jax.sharding import PartitionSpec as P

SUBSTEPS = 12
COURANT = 0.15
PRESSURE_GAIN = 0.1
CORIOLIS = 0.3
WAVE_MASS = 1.2
WAVE_MOMENTUM = 1.2
EPSILON = 1e-06


def extended_2(cells, sides, width, closed):
    for axis, dim in sides:
        count = lax.axis_size(axis)
        ends = count if closed else count - 1
        head = lax.slice_in_dim(cells, 0, width, axis=dim)
        tail = lax.slice_in_dim(cells, cells.shape[dim] - width, cells.shape[dim], axis=dim)
        cells = jnp.concatenate(
            [
                lax.ppermute(tail, axis, [(i, (i + 1) % count) for i in range(ends)]),
                cells,
                lax.ppermute(head, axis, [((i + 1) % count, i) for i in range(ends)]),
            ],
            axis=dim,
        )
    return cells


def weno_face(far_up, near_up, centre, near_down, far_down):
    poly_zero = (2.0 * far_up - 7.0 * near_up + 11.0 * centre) / 6.0
    poly_one = (-near_up + 5.0 * centre + 2.0 * near_down) / 6.0
    poly_two = (2.0 * centre + 5.0 * near_down - far_down) / 6.0
    smooth_zero = (
        13.0 / 12.0 * (far_up - 2.0 * near_up + centre) ** 2
        + 0.25 * (far_up - 4.0 * near_up + 3.0 * centre) ** 2
    )
    smooth_one = (
        13.0 / 12.0 * (near_up - 2.0 * centre + near_down) ** 2 + 0.25 * (near_up - near_down) ** 2
    )
    smooth_two = (
        13.0 / 12.0 * (centre - 2.0 * near_down + far_down) ** 2
        + 0.25 * (3.0 * centre - 4.0 * near_down + far_down) ** 2
    )
    weight_zero = 0.1 / (EPSILON + smooth_zero) ** 2
    weight_one = 0.6 / (EPSILON + smooth_one) ** 2
    weight_two = 0.3 / (EPSILON + smooth_two) ** 2
    return (weight_zero * poly_zero + weight_one * poly_one + weight_two * poly_two) / (
        weight_zero + weight_one + weight_two
    )


def face_fluxes(prognostic_bundle, velocity, wet_mask, along, length):

    def window(values, offset):
        return lax.slice_in_dim(values, offset, offset + length + 1, axis=along)

    face_speed = (
        0.5
        * (window(velocity, 2) + window(velocity, 3))
        * window(wet_mask, 2)
        * window(wet_mask, 3)
    )
    upwind = weno_face(
        window(prognostic_bundle, 0),
        window(prognostic_bundle, 1),
        window(prognostic_bundle, 2),
        window(prognostic_bundle, 3),
        window(prognostic_bundle, 4),
    )
    downwind = weno_face(
        window(prognostic_bundle, 5),
        window(prognostic_bundle, 4),
        window(prognostic_bundle, 3),
        window(prognostic_bundle, 2),
        window(prognostic_bundle, 1),
    )
    fluxes = COURANT * face_speed * jnp.where(face_speed >= 0.0, upwind, downwind)
    return (fluxes, face_speed)


def partner_fold(tops, parity, lead_offset, column_count, first_partner, northern, total_columns):
    facing = jnp.remainder(
        first_partner - lead_offset - lax.iota(jnp.int32, column_count), total_columns
    )
    picked = jnp.take(jnp.flip(tops, axis=1), facing, axis=2)
    return jnp.where(northern, parity * picked, 0.0)


def extend_deep(stacked_fields, parity, first_partner, northern, total_columns):
    channels, tile_rows, tile_cols = stacked_fields.shape
    east_west = extended_2(stacked_fields, (("lon", 2),), 3, True)
    north_south = extended_2(stacked_fields, (("lat", 1),), 3, False)
    tops = lax.all_gather(stacked_fields[:, tile_rows - 3 :, :], "lon", axis=2, tiled=True)
    ghosts = partner_fold(tops, parity, 0, tile_cols, first_partner, northern, total_columns)
    north_south = jnp.concatenate(
        [north_south[:, : tile_rows + 3], north_south[:, tile_rows + 3 :] + ghosts], axis=1
    )
    return (east_west, north_south)


def extend_wave(stacked_fields, margin, parity, first_partner, northern, total_columns):
    channels, tile_rows, tile_cols = stacked_fields.shape
    east_west = extended_2(stacked_fields, (("lon", 2),), margin, True)
    whole = extended_2(east_west, (("lat", 1),), margin, False)
    tops = lax.all_gather(stacked_fields[:, tile_rows - margin :, :], "lon", axis=2, tiled=True)
    ghosts = partner_fold(
        tops, parity, -margin, tile_cols + 2 * margin, first_partner, northern, total_columns
    )
    return jnp.concatenate(
        [whole[:, : tile_rows + margin], whole[:, tile_rows + margin :] + ghosts], axis=1
    )


def on_device(
    crosswise_speed_units,
    poleward_speed_units,
    thermal_anomaly,
    saltiness_anomaly,
    freeboard_elevation,
    barotropic_zonal_flow,
    barotropic_meridional_flow,
    submerged_layer_tally,
    seam_partner_index,
):
    levels, tile_rows, tile_cols = crosswise_speed_units.shape
    lat_size = lax.axis_size("lat")
    lon_size = lax.axis_size("lon")
    lat_index = lax.axis_index("lat")
    total_rows = tile_rows * lat_size
    total_columns = tile_cols * lon_size
    northern = lat_index == lat_size - 1
    first_partner = seam_partner_index[0]
    block_steps = 6
    margin = 2 * block_steps
    layer_total_real = submerged_layer_tally.astype(jnp.float32)
    stacked_fields = jnp.concatenate(
        [
            crosswise_speed_units,
            poleward_speed_units,
            thermal_anomaly,
            saltiness_anomaly,
            layer_total_real[None],
        ],
        axis=0,
    )
    parity = jnp.concatenate(
        [
            jnp.full((2 * levels, 1, 1), -1.0, jnp.float32),
            jnp.ones((2 * levels + 1, 1, 1), jnp.float32),
        ],
        axis=0,
    )
    east_west, north_south = extend_deep(
        stacked_fields, parity, first_partner, northern, total_columns
    )
    level_index = lax.broadcasted_iota(jnp.float32, (levels, 1, 1), 0)
    submerged_indicator = (level_index < layer_total_real[None]).astype(jnp.float32)
    wet_east = (level_index < east_west[4 * levels][None]).astype(jnp.float32)
    wet_north = (level_index < north_south[4 * levels][None]).astype(jnp.float32)
    fields_east = east_west[: 4 * levels].reshape(4, levels, tile_rows, tile_cols + 6)
    fields_north = north_south[: 4 * levels].reshape(4, levels, tile_rows + 6, tile_cols)
    flux_east, speed_east = face_fluxes(fields_east, fields_east[0:1], wet_east[None], 3, tile_cols)
    flux_north, speed_north = face_fluxes(
        fields_north, fields_north[1:2], wet_north[None], 2, tile_rows
    )
    prognostic_rate = -(flux_east[:, :, :, 1:] - flux_east[:, :, :, :-1]) - (
        flux_north[:, :, 1:, :] - flux_north[:, :, :-1, :]
    )
    spread = (
        speed_east[0, :, :, 1:]
        - speed_east[0, :, :, :-1]
        + (speed_north[0, :, 1:, :] - speed_north[0, :, :-1, :])
    )
    upward = -jnp.flip(jnp.cumsum(jnp.flip(spread, 0), axis=0), 0)
    prognostic_bundle = jnp.stack(
        [crosswise_speed_units, poleward_speed_units, thermal_anomaly, saltiness_anomaly], axis=0
    )
    interior = (
        COURANT * upward[None, 1:] * 0.5 * (prognostic_bundle[:, :-1] + prognostic_bundle[:, 1:])
    )
    boundary = jnp.zeros((4, 1, tile_rows, tile_cols), jnp.float32)
    vertical_flux = jnp.concatenate([boundary, interior, boundary], axis=1)
    prognostic_rate = prognostic_rate - (vertical_flux[:, :-1] - vertical_flux[:, 1:])
    density_east = 0.8 * fields_east[3] - 0.2 * fields_east[2]
    pressure_east = jnp.cumsum(density_east, axis=0) - 0.5 * density_east
    grad_east = 0.5 * (
        pressure_east[:, :, 4 : tile_cols + 4] - pressure_east[:, :, 2 : tile_cols + 2]
    )
    density_north = 0.8 * fields_north[3] - 0.2 * fields_north[2]
    pressure_north = jnp.cumsum(density_north, axis=0) - 0.5 * density_north
    grad_north = 0.5 * (
        pressure_north[:, 4 : tile_rows + 4, :] - pressure_north[:, 2 : tile_rows + 2, :]
    )
    own_rows = (lat_index * tile_rows + lax.iota(jnp.int32, tile_rows)).astype(jnp.float32)[:, None]
    coriolis = CORIOLIS * (2.0 * (own_rows + 0.5) / total_rows - 1.0)
    force_zonal = prognostic_rate[0] + coriolis * poleward_speed_units - PRESSURE_GAIN * grad_east
    force_merid = prognostic_rate[1] - coriolis * crosswise_speed_units - PRESSURE_GAIN * grad_north
    column = jnp.maximum(submerged_layer_tally, 1).astype(jnp.float32)
    mean_zonal = jnp.sum(submerged_indicator * force_zonal, axis=0) / column
    mean_merid = jnp.sum(submerged_indicator * force_merid, axis=0) / column
    static_parity = jnp.array([1.0, -1.0, -1.0], jnp.float32)[:, None, None]
    statics = extend_wave(
        jnp.stack([layer_total_real, mean_zonal, mean_merid], axis=0),
        margin,
        static_parity,
        first_partner,
        northern,
        total_columns,
    )
    thickness = statics[0] / levels
    wet_column = (statics[0] > 0.0).astype(jnp.float32)
    global_rows = lat_index * tile_rows - margin + lax.iota(jnp.int32, tile_rows + 2 * margin)
    mirrored = jnp.minimum(global_rows, 2 * total_rows - 1 - global_rows).astype(jnp.float32)[
        :, None
    ]
    coriolis_wide = CORIOLIS * (2.0 * (mirrored + 0.5) / total_rows - 1.0)

    def trim(values, keep):
        return values[
            margin - keep : margin + tile_rows + keep, margin - keep : margin + tile_cols + keep
        ]

    wave_parity = jnp.array([1.0, -1.0, -1.0], jnp.float32)[:, None, None]
    sea_level, zonal_flow, merid_flow = (
        freeboard_elevation,
        barotropic_zonal_flow,
        barotropic_meridional_flow,
    )
    for block in range(SUBSTEPS // block_steps):
        extended = extend_wave(
            jnp.stack([sea_level, zonal_flow, merid_flow], axis=0),
            margin,
            wave_parity,
            first_partner,
            northern,
            total_columns,
        )
        sea_level, zonal_flow, merid_flow = (extended[0], extended[1], extended[2])
        for inner_step in range(block_steps):
            outer = margin - 2 * inner_step
            keep = outer - 2
            thick = trim(thickness, outer)
            mass_east = thick * zonal_flow
            mass_north = thick * merid_flow
            spread_wave = 0.5 * (mass_east[1:-1, 2:] - mass_east[1:-1, :-2]) + 0.5 * (
                mass_north[2:, 1:-1] - mass_north[:-2, 1:-1]
            )
            next_level = trim(wet_column, outer - 1) * (
                sea_level[1:-1, 1:-1] - WAVE_MASS * spread_wave
            )
            rotation = coriolis_wide[margin - keep : margin + tile_rows + keep]
            wet_keep = trim(wet_column, keep)
            inner_zonal = zonal_flow[2:-2, 2:-2]
            inner_merid = merid_flow[2:-2, 2:-2]
            zonal_flow = wet_keep * (
                inner_zonal
                - WAVE_MOMENTUM * 0.5 * (next_level[1:-1, 2:] - next_level[1:-1, :-2])
                + (rotation * inner_merid + trim(statics[1], keep)) / SUBSTEPS
            )
            merid_flow = wet_keep * (
                inner_merid
                - WAVE_MOMENTUM * 0.5 * (next_level[2:, 1:-1] - next_level[:-2, 1:-1])
                + (-rotation * inner_zonal + trim(statics[2], keep)) / SUBSTEPS
            )
            sea_level = next_level[1:-1, 1:-1]
    zonal_speed_final = submerged_indicator * (
        crosswise_speed_units + force_zonal - mean_zonal + (zonal_flow - barotropic_zonal_flow)
    )
    poleward_speed_final = submerged_indicator * (
        poleward_speed_units + force_merid - mean_merid + (merid_flow - barotropic_meridional_flow)
    )
    thermal_final = submerged_indicator * (thermal_anomaly + prognostic_rate[2])
    saltiness_final = submerged_indicator * (saltiness_anomaly + prognostic_rate[3])
    return (
        zonal_speed_final,
        poleward_speed_final,
        thermal_final,
        saltiness_final,
        sea_level,
        zonal_flow,
        merid_flow,
    )


def solution(mesh):
    placed = (
        P(None, "lat", "lon"),
        P(None, "lat", "lon"),
        P(None, "lat", "lon"),
        P(None, "lat", "lon"),
        P("lat", "lon"),
        P("lat", "lon"),
        P("lat", "lon"),
        P("lat", "lon"),
        P("lon"),
    )
    return jax.shard_map(
        on_device,
        mesh=mesh,
        in_specs=placed,
        out_specs=(
            P(None, "lat", "lon"),
            P(None, "lat", "lon"),
            P(None, "lat", "lon"),
            P(None, "lat", "lon"),
            P("lat", "lon"),
            P("lat", "lon"),
            P("lat", "lon"),
        ),
        check_vma=False,
    )
```

profile of v0, /device:TPU:6, one launch (start us, length us, event | category | flops | bytes accessed | tf_op | source)
XLA Modules:
  0.0 298.3 jit_solution(17658706679827525291)
XLA Ops:
  8.2 3.0 %collective-permute-start.2 = (f32[33,3,256]{2,0,1:T(8,128)}, f32[33,3,256]{2,0,1:T(8,128)}, u32[]{:S(2)}, u32[]{:S(2)}) collective-permute-start(f32[33,3,256]{2,0,1:T(8,128)} %get-tuple-element.95), channel_id=1, source_target_pairs={{0,1},{1,2},{2,3},{4,5},{5,6},{6,7},{8,9},{9,10},{10,11},{12,13},{... | collective-permute-start | bytes 304136 | tf_op jit(solution)/shard_map/ppermute | solution.py:23
  13.3 4.6 %collective-permute-start.9 = (f32[3,16,12]{2,1,0:T(8,128)}, f32[3,16,12]{2,1,0:T(8,128)S(1)}, u32[]{:S(2)}, u32[]{:S(2)}) collective-permute-start(f32[3,16,12]{2,1,0:T(8,128)} %get-tuple-element.153), channel_id=1, source_target_pairs={{4,0},{8,4},{12,8},{16,12},{20,16},{24,20},{28,24},{0,28},{5,1},{9... | collective-permute-start | bytes 6920 | tf_op jit(solution)/shard_map/ppermute | solution.py:25
  17.9 33.4 %all_gather.12 = f32[33,3,2048]{2,0,1:T(8,128)S(1)} all-gather(f32[33,3,256]{2,0,1:T(8,128)} %get-tuple-element.95), channel_id=1, replica_groups=mesh['lon'=8,'lat'=4] {'lon'}, dimensions={2}, use_global_device_ids=true | all-gather | bytes 912384 | tf_op jit(solution)/shard_map/all_gather | solution.py:96
  60.5 31.6 %all_gather.14 = f32[3,12,2048]{2,1,0:T(8,128)S(1)} all-gather(f32[3,12,256]{2,1,0:T(8,128)} %slice.1172), channel_id=1, replica_groups=mesh['lon'=8,'lat'=4] {'lon'}, dimensions={2}, use_global_device_ids=true | all-gather | bytes 331776 | tf_op jit(solution)/shard_map/all_gather | solution.py:108
  93.3 3.1 %copy.196 = f32[33,3,2048]{0,1,2:T(4,128)} copy(f32[33,3,2048]{2,0,1:T(8,128)S(1)} %all_gather.12) | data formatting | bytes 1622016 | tf_op jit(solution)/shard_map/all_gather | solution.py:96
  96.4 11.6 %rev.21 = f32[33,3,2048]{0,1,2:T(4,128)} reverse(f32[33,3,2048]{0,1,2:T(4,128)} %copy.196), dimensions={1} | reverse | bytes 1622016 | tf_op jit(solution)/shard_map/jit(_flip)/rev | solution.py:88
  108.1 3.2 %gather_fusion = f32[256,33,3]{1,2,0:T(4,128)S(1)} fusion(f32[33,3,2048]{0,1,2:T(4,128)} %rev.21, s32[1024]{0:T(1024)S(1)} %pad_clamp_fusion.1), kind=kCustom, calls=%fused_computation.3 | custom fusion | bytes 203776 | tf_op jit(solution)/shard_map/jit(_take)/gather | solution.py:88
  112.1 3.2 %copy.214 = f32[3,12,2048]{1,0,2:T(4,128)} copy(f32[3,12,2048]{2,1,0:T(8,128)S(1)} %all_gather.14) | data formatting | bytes 589824 | tf_op jit(solution)/shard_map/all_gather | solution.py:108
  115.3 12.0 %rev.25 = f32[3,12,2048]{1,0,2:T(4,128)} reverse(f32[3,12,2048]{1,0,2:T(4,128)} %copy.214), dimensions={1} | reverse | bytes 589824 | tf_op jit(solution)/shard_map/jit(_flip)/rev | solution.py:88
  127.2 4.1 %gather_fusion.2 = f32[280,3,12]{2,1,0:T(4,128)} fusion(f32[3,12,2048]{1,0,2:T(4,128)} %rev.25, s32[1024]{0:T(1024)S(1)} %pad_clamp_fusion), kind=kCustom, calls=%fused_computation.1.clone | custom fusion | bytes 81760 | tf_op jit(solution)/shard_map/jit(_take)/gather | solution.py:88
  134.8 3.2 %collective-permute-start.10 = (f32[3,12,280]{2,1,0:T(8,128)}, f32[3,12,280]{2,1,0:T(8,128)}, u32[]{:S(2)}, u32[]{:S(2)}) collective-permute-start(f32[3,12,280]{2,1,0:T(8,128)} %get-tuple-element.146), channel_id=1, source_target_pairs={{0,1},{1,2},{2,3},{4,5},{5,6},{6,7},{8,9},{9,10},{10,11},{12,13},{... | collective-permute-start | bytes 120968 | tf_op jit(solution)/shard_map/ppermute | solution.py:23
  138.4 2.7 fusion.254
  143.5 5.4 %select_multiply_fusion = f32[4,8,16,257]{3,1,2,0:T(8,128)S(1)} fusion(f32[4,8,16,257]{3,2,1,0:T(8,128)} %get-tuple-element.88, f32[4,8,16,257]{3,2,1,0:T(8,128)S(1)} %get-tuple-element.84, f32[4,8,16,257]{3,2,1,0:T(8,128)} %get-tuple-element.85, f32[4,8,16,257]{3,2,1,0:T(8,128)} %get-tuple-element.86, f32[4,8,16,257]{3,2,1,0:T(8,128)} %get-tuple-element.87, ...), kind=kLoop, calls=%fused_computation.6 | loop fusion | flops 16579584 | bytes 3848832 | tf_op jit(solution)/shard_map/mul | solution.py:80
  158.8 3.7 %select_multiply_fusion.1 = f32[4,8,17,256]{3,1,2,0:T(8,128)S(1)} fusion(f32[4,8,17,256]{3,1,0,2:T(8,128)} %get-tuple-element.94, f32[4,8,17,256]{3,1,0,2:T(8,128)S(1)} %get-tuple-element.90, f32[4,8,17,256]{3,1,0,2:T(8,128)} %get-tuple-element.91, f32[4,8,17,256]{3,1,0,2:T(8,128)} %get-tuple-element.92, f32[4,8,17,256]{3,1,0,2:T(8,128)} %get-tuple-element.93, ...), kind=kLoop, calls=%fused_computation.40 | loop fusion | flops 17547264 | bytes 4073472 | tf_op jit(solution)/shard_map/mul | solution.py:80
  163.4 3.5 %collective-permute-start.5 = (f32[3,16,12]{2,1,0:T(8,128)S(1)}, f32[3,16,12]{2,1,0:T(8,128)S(1)}, u32[]{:S(2)}, u32[]{:S(2)}) collective-permute-start(f32[3,16,12]{2,1,0:T(8,128)S(1)} %get-tuple-element.155), channel_id=1, source_target_pairs={{4,0},{8,4},{12,8},{16,12},{20,16},{24,20},{28,24},{0,28},{5,1},{9... | collective-permute-start | bytes 6920 | tf_op jit(solution)/shard_map/ppermute | solution.py:25
  166.9 33.2 %all_gather.13 = f32[3,12,2048]{2,1,0:T(8,128)S(1)} all-gather(f32[3,12,256]{2,1,0:T(8,128)S(1)} %slice.1154), channel_id=1, replica_groups=mesh['lon'=8,'lat'=4] {'lon'}, dimensions={2}, use_global_device_ids=true | all-gather | bytes 331776 | tf_op jit(solution)/shard_map/all_gather | solution.py:108
  200.1 3.1 %copy.212 = f32[3,12,2048]{1,0,2:T(4,128)} copy(f32[3,12,2048]{2,1,0:T(8,128)S(1)} %all_gather.13) | data formatting | bytes 589824 | tf_op jit(solution)/shard_map/all_gather | solution.py:108
  203.3 12.0 %rev.24 = f32[3,12,2048]{1,0,2:T(4,128)} reverse(f32[3,12,2048]{1,0,2:T(4,128)} %copy.212), dimensions={1} | reverse | bytes 589824 | tf_op jit(solution)/shard_map/jit(_flip)/rev | solution.py:88
  215.3 3.3 %gather_fusion.1 = f32[280,3,12]{2,1,0:T(4,128)S(1)} fusion(f32[3,12,2048]{1,0,2:T(4,128)} %rev.24, s32[1024]{0:T(1024)S(1)} %copy-done.29), kind=kCustom, calls=%fused_computation.clone | custom fusion | bytes 81760 | tf_op jit(solution)/shard_map/jit(_take)/gather | solution.py:88
  232.2 2.9 collective-permute-start.12
  235.1 32.8 %all_gather.15 = f32[3,12,2048]{2,1,0:T(8,128)S(1)} all-gather(f32[3,12,256]{2,1,0:T(8,128)S(1)} %slice.1266), channel_id=1, replica_groups=mesh['lon'=8,'lat'=4] {'lon'}, dimensions={2}, use_global_device_ids=true | all-gather | bytes 331776 | tf_op jit(solution)/shard_map/all_gather | solution.py:108
  267.9 3.1 %copy.216 = f32[3,12,2048]{1,0,2:T(4,128)} copy(f32[3,12,2048]{2,1,0:T(8,128)S(1)} %all_gather.15) | data formatting | bytes 589824 | tf_op jit(solution)/shard_map/all_gather | solution.py:108
  271.0 12.0 %rev.26 = f32[3,12,2048]{1,0,2:T(4,128)} reverse(f32[3,12,2048]{1,0,2:T(4,128)} %copy.216), dimensions={1} | reverse | bytes 589824 | tf_op jit(solution)/shard_map/jit(_flip)/rev | solution.py:88
  283.0 3.2 %gather_fusion.3 = f32[280,3,12]{2,1,0:T(4,128)S(1)} fusion(f32[3,12,2048]{1,0,2:T(4,128)} %rev.26, s32[1024]{0:T(1024)S(1)} %copy-done.29), kind=kCustom, calls=%fused_computation.2.clone | custom fusion | bytes 81760 | tf_op jit(solution)/shard_map/jit(_take)/gather | solution.py:88
  (245 shorter events, 62.0 us)
Async XLA Ops:
  0.6 58.8 %copy-start.4 = (f32[8,16,256]{2,1,0:T(8,128)S(1)}, f32[8,16,256]{2,1,0:T(8,128)}, u32[]{:S(2)}) copy-start(f32[8,16,256]{2,1,0:T(8,128)} %param.13) | copy-start | bytes 393220
  0.6 58.7 %copy-start.6 = (f32[8,16,256]{2,1,0:T(8,128)S(1)}, f32[8,16,256]{2,1,0:T(8,128)}, u32[]{:S(2)}) copy-start(f32[8,16,256]{2,1,0:T(8,128)} %param.14) | copy-start | bytes 393220
  0.7 58.7 %copy-start.8 = (f32[8,16,256]{2,1,0:T(8,128)S(1)}, f32[8,16,256]{2,1,0:T(8,128)}, u32[]{:S(2)}) copy-start(f32[8,16,256]{2,1,0:T(8,128)} %param.15) | copy-start | bytes 393220
  0.7 58.7 %copy-start.10 = (f32[8,16,256]{2,1,0:T(8,128)S(1)}, f32[8,16,256]{2,1,0:T(8,128)}, u32[]{:S(2)}) copy-start(f32[8,16,256]{2,1,0:T(8,128)} %param.16) | copy-start | bytes 393220
  0.7 52.9 %copy-start.22 = (s32[16,256]{1,0:T(8,128)S(1)}, s32[16,256]{1,0:T(8,128)}, u32[]{:S(2)}) copy-start(s32[16,256]{1,0:T(8,128)} %param.20) | copy-start | bytes 49156
  0.7 50.6 %copy-start.47 = (s32[256]{0:T(256)S(1)}, s32[256]{0:T(256)}, u32[]{:S(2)}) copy-start(s32[256]{0:T(256)} %param.21) | copy-start | bytes 3076
  6.2 142.7 %collective-permute-start.3 = (f32[33,3,256]{2,0,1:T(8,128)}, f32[33,3,256]{2,0,1:T(8,128)}, u32[]{:S(2)}, u32[]{:S(2)}) collective-permute-start(f32[33,3,256]{2,0,1:T(8,128)} %get-tuple-element.96), channel_id=1, source_target_pairs={{1,0},{2,1},{3,2},{5,4},{6,5},{7,6},{9,8},{10,9},{11,10},{13,12},{... | collective-permute-start | bytes 304136 | tf_op jit(solution)/shard_map/ppermute | solution.py:25
  8.2 141.9 %collective-permute-start.2 = (f32[33,3,256]{2,0,1:T(8,128)}, f32[33,3,256]{2,0,1:T(8,128)}, u32[]{:S(2)}, u32[]{:S(2)}) collective-permute-start(f32[33,3,256]{2,0,1:T(8,128)} %get-tuple-element.95), channel_id=1, source_target_pairs={{0,1},{1,2},{2,3},{4,5},{5,6},{6,7},{8,9},{9,10},{10,11},{12,13},{... | collective-permute-start | bytes 304136 | tf_op jit(solution)/shard_map/ppermute | solution.py:23
  11.3 123.4 %collective-permute-start.1 = (f32[33,16,3]{2,1,0:T(8,128)S(1)}, f32[33,16,3]{2,1,0:T(8,128)S(1)}, u32[]{:S(2)}, u32[]{:S(2)}) collective-permute-start(f32[33,16,3]{2,1,0:T(8,128)S(1)} %get-tuple-element.104), channel_id=1, source_target_pairs={{4,0},{8,4},{12,8},{16,12},{20,16},{24,20},{28,24},{0,28},{5,1},{9... | collective-permute-start | bytes 19016 | tf_op jit(solution)/shard_map/ppermute | solution.py:25
  13.3 118.0 %collective-permute-start.9 = (f32[3,16,12]{2,1,0:T(8,128)}, f32[3,16,12]{2,1,0:T(8,128)S(1)}, u32[]{:S(2)}, u32[]{:S(2)}) collective-permute-start(f32[3,16,12]{2,1,0:T(8,128)} %get-tuple-element.153), channel_id=1, source_target_pairs={{4,0},{8,4},{12,8},{16,12},{20,16},{24,20},{28,24},{0,28},{5,1},{9... | collective-permute-start | bytes 6920 | tf_op jit(solution)/shard_map/ppermute | solution.py:25
  17.9 113.4 %collective-permute-start.8 = (f32[3,16,12]{2,1,0:T(8,128)}, f32[3,16,12]{2,1,0:T(8,128)}, u32[]{:S(2)}, u32[]{:S(2)}) collective-permute-start(f32[3,16,12]{2,1,0:T(8,128)} %get-tuple-element.152), channel_id=1, source_target_pairs={{0,4},{4,8},{8,12},{12,16},{16,20},{20,24},{24,28},{28,0},{1,5},{5... | collective-permute-start | bytes 6920 | tf_op jit(solution)/shard_map/ppermute | solution.py:23
  92.7 34.5 %copy-start.28 = (s32[1024]{0:T(1024)}, s32[1024]{0:T(1024)S(1)}, u32[]{:S(2)}) copy-start(s32[1024]{0:T(1024)S(1)} %pad_clamp_fusion) | copy-start | bytes 12292
  131.3 6.7 %collective-permute-start = (f32[33,16,3]{2,1,0:T(8,128)S(1)}, f32[33,16,3]{2,1,0:T(8,128)S(1)}, u32[]{:S(2)}, u32[]{:S(2)}) collective-permute-start(f32[33,16,3]{2,1,0:T(8,128)S(1)} %get-tuple-element.103), channel_id=1, source_target_pairs={{0,4},{4,8},{8,12},{12,16},{16,20},{20,24},{24,28},{28,0},{1,5},{5... | collective-permute-start | bytes 19016 | tf_op jit(solution)/shard_map/ppermute | solution.py:23
  132.8 87.1 %collective-permute-start.11 = (f32[3,12,280]{2,1,0:T(8,128)}, f32[3,12,280]{2,1,0:T(8,128)}, u32[]{:S(2)}, u32[]{:S(2)}) collective-permute-start(f32[3,12,280]{2,1,0:T(8,128)} %get-tuple-element.147), channel_id=1, source_target_pairs={{1,0},{2,1},{3,2},{5,4},{6,5},{7,6},{9,8},{10,9},{11,10},{13,12},{... | collective-permute-start | bytes 120968 | tf_op jit(solution)/shard_map/ppermute | solution.py:25
  134.8 86.1 %collective-permute-start.10 = (f32[3,12,280]{2,1,0:T(8,128)}, f32[3,12,280]{2,1,0:T(8,128)}, u32[]{:S(2)}, u32[]{:S(2)}) collective-permute-start(f32[3,12,280]{2,1,0:T(8,128)} %get-tuple-element.146), channel_id=1, source_target_pairs={{0,1},{1,2},{2,3},{4,5},{5,6},{6,7},{8,9},{9,10},{10,11},{12,13},{... | collective-permute-start | bytes 120968 | tf_op jit(solution)/shard_map/ppermute | solution.py:23
  163.4 58.6 %collective-permute-start.5 = (f32[3,16,12]{2,1,0:T(8,128)S(1)}, f32[3,16,12]{2,1,0:T(8,128)S(1)}, u32[]{:S(2)}, u32[]{:S(2)}) collective-permute-start(f32[3,16,12]{2,1,0:T(8,128)S(1)} %get-tuple-element.155), channel_id=1, source_target_pairs={{4,0},{8,4},{12,8},{16,12},{20,16},{24,20},{28,24},{0,28},{5,1},{9... | collective-permute-start | bytes 6920 | tf_op jit(solution)/shard_map/ppermute | solution.py:25
  166.9 55.1 %collective-permute-start.4 = (f32[3,16,12]{2,1,0:T(8,128)S(1)}, f32[3,16,12]{2,1,0:T(8,128)S(1)}, u32[]{:S(2)}, u32[]{:S(2)}) collective-permute-start(f32[3,16,12]{2,1,0:T(8,128)S(1)} %get-tuple-element.154), channel_id=1, source_target_pairs={{0,4},{4,8},{8,12},{12,16},{16,20},{20,24},{24,28},{28,0},{1,5},{5... | collective-permute-start | bytes 6920 | tf_op jit(solution)/shard_map/ppermute | solution.py:23
  203.3 18.7 %copy-start.19 = (f32[1,16,256]{2,1,0:T(8,128)S(1)}, f32[1,16,256]{2,1,0:T(8,128)}, u32[]{:S(2)}) copy-start(f32[1,16,256]{2,1,0:T(8,128)} %get-tuple-element.160) | copy-start | bytes 49156
  222.1 6.3 %collective-permute-start.7 = (f32[3,12,280]{2,1,0:T(8,128)S(1)}, f32[3,12,280]{2,1,0:T(8,128)S(1)}, u32[]{:S(2)}, u32[]{:S(2)}) collective-permute-start(f32[3,12,280]{2,1,0:T(8,128)S(1)} %get-tuple-element.149), channel_id=1, source_target_pairs={{1,0},{2,1},{3,2},{5,4},{6,5},{7,6},{9,8},{10,9},{11,10},{13,12},{... | collective-permute-start | bytes 120968 | tf_op jit(solution)/shard_map/ppermute | solution.py:25
  224.1 5.7 %collective-permute-start.6 = (f32[3,12,280]{2,1,0:T(8,128)S(1)}, f32[3,12,280]{2,1,0:T(8,128)S(1)}, u32[]{:S(2)}, u32[]{:S(2)}) collective-permute-start(f32[3,12,280]{2,1,0:T(8,128)S(1)} %get-tuple-element.148), channel_id=1, source_target_pairs={{0,1},{1,2},{2,3},{4,5},{5,6},{6,7},{8,9},{9,10},{10,11},{12,13},{... | collective-permute-start | bytes 120968 | tf_op jit(solution)/shard_map/ppermute | solution.py:23
  232.1 54.1 %collective-permute-start.13 = (f32[3,16,12]{2,1,0:T(8,128)S(1)}, f32[3,16,12]{2,1,0:T(8,128)S(1)}, u32[]{:S(2)}, u32[]{:S(2)}) collective-permute-start(f32[3,16,12]{2,1,0:T(8,128)S(1)} %get-tuple-element.151), channel_id=1, source_target_pairs={{4,0},{8,4},{12,8},{16,12},{20,16},{24,20},{28,24},{0,28},{5,1},{9... | collective-permute-start | bytes 6920 | tf_op jit(solution)/shard_map/ppermute | solution.py:25
  232.2 54.0 %collective-permute-start.12 = (f32[3,16,12]{2,1,0:T(8,128)S(1)}, f32[3,16,12]{2,1,0:T(8,128)S(1)}, u32[]{:S(2)}, u32[]{:S(2)}) collective-permute-start(f32[3,16,12]{2,1,0:T(8,128)S(1)} %get-tuple-element.150), channel_id=1, source_target_pairs={{0,4},{4,8},{8,12},{12,16},{16,20},{20,24},{24,28},{28,0},{1,5},{5... | collective-permute-start | bytes 6920 | tf_op jit(solution)/shard_map/ppermute | solution.py:23
  286.3 5.6 %collective-permute-start.15 = (f32[3,12,280]{2,1,0:T(8,128)S(1)}, f32[3,12,280]{2,1,0:T(8,128)S(1)}, u32[]{:S(2)}, u32[]{:S(2)}) collective-permute-start(f32[3,12,280]{2,1,0:T(8,128)S(1)} %get-tuple-element.145), channel_id=1, source_target_pairs={{1,0},{2,1},{3,2},{5,4},{6,5},{7,6},{9,8},{10,9},{11,10},{13,12},{... | collective-permute-start | bytes 120968 | tf_op jit(solution)/shard_map/ppermute | solution.py:25
  288.3 5.7 %collective-permute-start.14 = (f32[3,12,280]{2,1,0:T(8,128)S(1)}, f32[3,12,280]{2,1,0:T(8,128)S(1)}, u32[]{:S(2)}, u32[]{:S(2)}) collective-permute-start(f32[3,12,280]{2,1,0:T(8,128)S(1)} %get-tuple-element.144), channel_id=1, source_target_pairs={{0,1},{1,2},{2,3},{4,5},{5,6},{6,7},{8,9},{9,10},{10,11},{12,13},{... | collective-permute-start | bytes 120968 | tf_op jit(solution)/shard_map/ppermute | solution.py:23
  (40 other events, 402.1 us)
where the time goes:
time: 301 us; the launch traced here: 298 us
  blocking collectives  131 us (44%)
  local copies, waits for them, and re-layouts  91.7 us (30%)
  other arithmetic  39.2 us (13%)
  starting transfers between devices  30.5 us (10%)
  waiting for transfers between devices  3.36 us (1%)
    all_gather x3, blocking collectives, extend_wave(): lax.all_gather(stacked_fields[:, tile_rows - margin:, :], 'lon', axis=2,...  97.6 us
    rev x4, local copies, waits for them, and re-layouts, partner_fold(): picked = jnp.take(jnp.flip(tops, axis=1), facing, axis=2)  47.5 us
    all_gather x1, blocking collectives, extend_deep(): lax.all_gather(stacked_fields[:, tile_rows - 3:, :], 'lon', axis=2, tiled...  33.4 us
    ppermute x8, starting transfers between devices, extended_2(): lax.ppermute(head, axis, [((i + 1) % count, i) for i in range(ends)])  16.4 us
    gather x5, local copies, waits for them, and re-layouts, partner_fold(): picked = jnp.take(jnp.flip(tops, axis=1), facing, axis=2)  14.6 us
    ppermute x8, starting transfers between devices, extended_2(): lax.ppermute(tail, axis, [(i, (i + 1) % count) for i in range(ends)])  14.1 us
    mul x4, other arithmetic, face_fluxes(): COURANT * face_speed * jnp.where(face_speed >= 0.0, upwind, downwind)  10.5 us
    all_gather x3, local copies, waits for them, and re-layouts, extend_wave(): lax.all_gather(stacked_fields[:, tile_rows - margin:, :], 'lon', axis=2,...  9.4 us
  transfers between devices with their start and end apart: 16, of which 2 were waited for; matrix products, arithmetic and copies ran while one was open for 40% of the time, Pallas kernels for 0%

commit v1 on v0

--- a/solution.py
+++ b/solution.py
@@ -105,7 +105,9 @@
     channels, tile_rows, tile_cols = stacked_fields.shape
     east_west = extended_2(stacked_fields, (("lon", 2),), margin, True)
     whole = extended_2(east_west, (("lat", 1),), margin, False)
-    tops = lax.all_gather(stacked_fields[:, tile_rows - margin :, :], "lon", axis=2, tiled=True)
+    part = stacked_fields[:, tile_rows - margin :, :]
+    parts = lax.all_gather(part, "lon")
+    tops = jnp.concatenate(parts, axis=2)
     ghosts = partner_fold(
         tops, parity, -margin, tile_cols + 2 * margin, first_partner, northern, total_columns
     )

time: 301 us -> 300 us (level)
    all_gather x3 -> x0, local copies, waits for them, and re-layouts: 9.4 us -> none  [extend_wave(): lax.all_gather(stacked_fields[:, tile_rows - margin:, :], 'lon', axis=2,...]
    reshape x0 -> x3, local copies, waits for them, and re-layouts: none -> 9.39 us  [extend_wave(): tops = jnp.concatenate(parts, axis=2)]
where the time goes in v1:
time: 300 us; the launch traced here: 298 us
  blocking collectives  131 us (44%)
  local copies, waits for them, and re-layouts  91.7 us (31%)
  other arithmetic  39.2 us (13%)
  starting transfers between devices  30.5 us (10%)
  waiting for transfers between devices  3.36 us (1%)
    all_gather x3, blocking collectives, extend_wave(): parts = lax.all_gather(part, 'lon')  97.6 us
    rev x4, local copies, waits for them, and re-layouts, partner_fold(): picked = jnp.take(jnp.flip(tops, axis=1), facing, axis=2)  47.5 us
    all_gather x1, blocking collectives, extend_deep(): lax.all_gather(stacked_fields[:, tile_rows - 3:, :], 'lon', axis=2, tiled...  33.4 us
    ppermute x8, starting transfers between devices, extended_2(): lax.ppermute(head, axis, [((i + 1) % count, i) for i in range(ends)])  16.4 us
    gather x5, local copies, waits for them, and re-layouts, partner_fold(): picked = jnp.take(jnp.flip(tops, axis=1), facing, axis=2)  14.6 us
    ppermute x8, starting transfers between devices, extended_2(): lax.ppermute(tail, axis, [(i, (i + 1) % count) for i in range(ends)])  14.1 us
    mul x4, other arithmetic, face_fluxes(): COURANT * face_speed * jnp.where(face_speed >= 0.0, upwind, downwind)  10.5 us
    reshape x3, local copies, waits for them, and re-layouts, extend_wave(): tops = jnp.concatenate(parts, axis=2)  9.39 us
  transfers between devices with their start and end apart: 16, of which 2 were waited for; matrix products, arithmetic and copies ran while one was open for 40% of the time, Pallas kernels for 0%

profile of v1, /device:TPU:6, one launch (start us, length us, event | category | flops | bytes accessed | tf_op | source)
XLA Modules:
  0.0 298.3 jit_solution(12981026127346943061)
XLA Ops:
  8.2 3.0 %collective-permute-start.2 = (f32[33,3,256]{2,0,1:T(8,128)}, f32[33,3,256]{2,0,1:T(8,128)}, u32[]{:S(2)}, u32[]{:S(2)}) collective-permute-start(f32[33,3,256]{2,0,1:T(8,128)} %get-tuple-element.95), channel_id=1, source_target_pairs={{0,1},{1,2},{2,3},{4,5},{5,6},{6,7},{8,9},{9,10},{10,11},{12,13},{... | collective-permute-start | bytes 304136 | tf_op jit(solution)/shard_map/ppermute | solution.py:23
  13.3 4.6 %collective-permute-start.9 = (f32[3,16,12]{2,1,0:T(8,128)}, f32[3,16,12]{2,1,0:T(8,128)S(1)}, u32[]{:S(2)}, u32[]{:S(2)}) collective-permute-start(f32[3,16,12]{2,1,0:T(8,128)} %get-tuple-element.153), channel_id=1, source_target_pairs={{4,0},{8,4},{12,8},{16,12},{20,16},{24,20},{28,24},{0,28},{5,1},{9... | collective-permute-start | bytes 6920 | tf_op jit(solution)/shard_map/ppermute | solution.py:25
  17.9 33.4 %all_gather.21 = f32[33,3,2048]{2,0,1:T(8,128)S(1)} all-gather(f32[33,3,256]{2,0,1:T(8,128)} %get-tuple-element.95), channel_id=1, replica_groups=mesh['lon'=8,'lat'=4] {'lon'}, dimensions={2}, use_global_device_ids=true | all-gather | bytes 912384 | tf_op jit(solution)/shard_map/all_gather | solution.py:96
  60.5 31.6 %all-gather.1 = f32[24,12,256]{2,1,0:T(8,128)S(1)} all-gather(f32[3,12,256]{2,1,0:T(8,128)} %slice.1172), channel_id=3, replica_groups=mesh['lon'=8,'lat'=4] {'lon'}, dimensions={0}, use_global_device_ids=true | all-gather | bytes 331776 | tf_op jit(solution)/shard_map/all_gather | solution.py:109
  93.3 3.1 %copy.216 = f32[33,3,2048]{0,1,2:T(4,128)} copy(f32[33,3,2048]{2,0,1:T(8,128)S(1)} %all_gather.21) | data formatting | bytes 1622016 | tf_op jit(solution)/shard_map/all_gather | solution.py:96
  96.4 11.6 %rev.21 = f32[33,3,2048]{0,1,2:T(4,128)} reverse(f32[33,3,2048]{0,1,2:T(4,128)} %copy.216), dimensions={1} | reverse | bytes 1622016 | tf_op jit(solution)/shard_map/jit(_flip)/rev | solution.py:88
  108.1 3.2 %gather_fusion = f32[256,33,3]{1,2,0:T(4,128)S(1)} fusion(f32[33,3,2048]{0,1,2:T(4,128)} %rev.21, s32[1024]{0:T(1024)S(1)} %pad_clamp_fusion.1), kind=kCustom, calls=%fused_computation.3 | custom fusion | bytes 203776 | tf_op jit(solution)/shard_map/jit(_take)/gather | solution.py:88
  112.1 3.2 %copy.251 = f32[3,12,8,256]{1,0,3,2:T(4,128)} copy(f32[3,12,8,256]{3,1,0,2:T(8,128)S(1)} %bitcast.165) | data formatting | bytes 589824 | tf_op jit(solution)/shard_map/reshape | solution.py:110
  115.3 12.0 %rev.25 = f32[3,12,2048]{1,0,2:T(4,128)} reverse(f32[3,12,2048]{1,0,2:T(4,128)} %bitcast.159), dimensions={1} | reverse | bytes 589824 | tf_op jit(solution)/shard_map/jit(_flip)/rev | solution.py:88
  127.2 4.1 %gather_fusion.2 = f32[280,3,12]{2,1,0:T(4,128)} fusion(f32[3,12,2048]{1,0,2:T(4,128)} %rev.25, s32[1024]{0:T(1024)S(1)} %pad_clamp_fusion), kind=kCustom, calls=%fused_computation.1.clone | custom fusion | bytes 81760 | tf_op jit(solution)/shard_map/jit(_take)/gather | solution.py:88
  134.8 3.2 %collective-permute-start.10 = (f32[3,12,280]{2,1,0:T(8,128)}, f32[3,12,280]{2,1,0:T(8,128)}, u32[]{:S(2)}, u32[]{:S(2)}) collective-permute-start(f32[3,12,280]{2,1,0:T(8,128)} %get-tuple-element.146), channel_id=1, source_target_pairs={{0,1},{1,2},{2,3},{4,5},{5,6},{6,7},{8,9},{9,10},{10,11},{12,13},{... | collective-permute-start | bytes 120968 | tf_op jit(solution)/shard_map/ppermute | solution.py:23
  138.4 2.7 fusion.254
  143.5 5.4 %select_multiply_fusion = f32[4,8,16,257]{3,1,2,0:T(8,128)S(1)} fusion(f32[4,8,16,257]{3,2,1,0:T(8,128)} %get-tuple-element.88, f32[4,8,16,257]{3,2,1,0:T(8,128)S(1)} %get-tuple-element.84, f32[4,8,16,257]{3,2,1,0:T(8,128)} %get-tuple-element.85, f32[4,8,16,257]{3,2,1,0:T(8,128)} %get-tuple-element.86, f32[4,8,16,257]{3,2,1,0:T(8,128)} %get-tuple-element.87, ...), kind=kLoop, calls=%fused_computation.6 | loop fusion | flops 16579584 | bytes 3848832 | tf_op jit(solution)/shard_map/mul | solution.py:80
  158.8 3.7 %select_multiply_fusion.1 = f32[4,8,17,256]{3,1,2,0:T(8,128)S(1)} fusion(f32[4,8,17,256]{3,1,0,2:T(8,128)} %get-tuple-element.94, f32[4,8,17,256]{3,1,0,2:T(8,128)S(1)} %get-tuple-element.90, f32[4,8,17,256]{3,1,0,2:T(8,128)} %get-tuple-element.91, f32[4,8,17,256]{3,1,0,2:T(8,128)} %get-tuple-element.92, f32[4,8,17,256]{3,1,0,2:T(8,128)} %get-tuple-element.93, ...), kind=kLoop, calls=%fused_computation.40 | loop fusion | flops 17547264 | bytes 4073472 | tf_op jit(solution)/shard_map/mul | solution.py:80
  163.4 3.5 %collective-permute-start.5 = (f32[3,16,12]{2,1,0:T(8,128)S(1)}, f32[3,16,12]{2,1,0:T(8,128)S(1)}, u32[]{:S(2)}, u32[]{:S(2)}) collective-permute-start(f32[3,16,12]{2,1,0:T(8,128)S(1)} %get-tuple-element.155), channel_id=1, source_target_pairs={{4,0},{8,4},{12,8},{16,12},{20,16},{24,20},{28,24},{0,28},{5,1},{9... | collective-permute-start | bytes 6920 | tf_op jit(solution)/shard_map/ppermute | solution.py:25
  166.9 33.2 %all-gather = f32[24,12,256]{2,1,0:T(8,128)S(1)} all-gather(f32[3,12,256]{2,1,0:T(8,128)S(1)} %slice.1154), channel_id=2, replica_groups=mesh['lon'=8,'lat'=4] {'lon'}, dimensions={0}, use_global_device_ids=true | all-gather | bytes 331776 | tf_op jit(solution)/shard_map/all_gather | solution.py:109
  200.1 3.1 %copy.256 = f32[8,3,12,256]{2,1,3,0:T(4,128)} copy(f32[8,3,12,256]{3,2,1,0:T(8,128)S(1)} %bitcast.166) | data formatting | bytes 589824 | tf_op jit(solution)/shard_map/reshape | solution.py:110
  203.3 12.0 %rev.24 = f32[3,12,2048]{1,0,2:T(4,128)} reverse(f32[3,12,2048]{1,0,2:T(4,128)} %bitcast.160), dimensions={1} | reverse | bytes 589824 | tf_op jit(solution)/shard_map/jit(_flip)/rev | solution.py:88
  215.3 3.3 %gather_fusion.1 = f32[280,3,12]{2,1,0:T(4,128)S(1)} fusion(f32[3,12,2048]{1,0,2:T(4,128)} %rev.24, s32[1024]{0:T(1024)S(1)} %copy-done.29), kind=kCustom, calls=%fused_computation.clone | custom fusion | bytes 81760 | tf_op jit(solution)/shard_map/jit(_take)/gather | solution.py:88
  232.2 2.9 collective-permute-start.12
  235.1 32.8 %all-gather.2 = f32[24,12,256]{2,1,0:T(8,128)S(1)} all-gather(f32[3,12,256]{2,1,0:T(8,128)S(1)} %slice.1266), channel_id=4, replica_groups=mesh['lon'=8,'lat'=4] {'lon'}, dimensions={0}, use_global_device_ids=true | all-gather | bytes 331776 | tf_op jit(solution)/shard_map/all_gather | solution.py:109
  267.9 3.1 %copy.252 = f32[3,12,8,256]{1,0,3,2:T(4,128)} copy(f32[3,12,8,256]{3,1,0,2:T(8,128)S(1)} %bitcast.167) | data formatting | bytes 589824 | tf_op jit(solution)/shard_map/reshape | solution.py:110
  271.0 12.0 %rev.26 = f32[3,12,2048]{1,0,2:T(4,128)} reverse(f32[3,12,2048]{1,0,2:T(4,128)} %bitcast.161), dimensions={1} | reverse | bytes 589824 | tf_op jit(solution)/shard_map/jit(_flip)/rev | solution.py:88
  282.9 3.2 %gather_fusion.3 = f32[280,3,12]{2,1,0:T(4,128)S(1)} fusion(f32[3,12,2048]{1,0,2:T(4,128)} %rev.26, s32[1024]{0:T(1024)S(1)} %copy-done.29), kind=kCustom, calls=%fused_computation.2.clone | custom fusion | bytes 81760 | tf_op jit(solution)/shard_map/jit(_take)/gather | solution.py:88
  (245 shorter events, 62.0 us)
Async XLA Ops:
  0.6 58.8 %copy-start.4 = (f32[8,16,256]{2,1,0:T(8,128)S(1)}, f32[8,16,256]{2,1,0:T(8,128)}, u32[]{:S(2)}) copy-start(f32[8,16,256]{2,1,0:T(8,128)} %param.13) | copy-start | bytes 393220
  0.6 58.7 %copy-start.6 = (f32[8,16,256]{2,1,0:T(8,128)S(1)}, f32[8,16,256]{2,1,0:T(8,128)}, u32[]{:S(2)}) copy-start(f32[8,16,256]{2,1,0:T(8,128)} %param.14) | copy-start | bytes 393220
  0.7 58.7 %copy-start.8 = (f32[8,16,256]{2,1,0:T(8,128)S(1)}, f32[8,16,256]{2,1,0:T(8,128)}, u32[]{:S(2)}) copy-start(f32[8,16,256]{2,1,0:T(8,128)} %param.15) | copy-start | bytes 393220
  0.7 58.7 %copy-start.10 = (f32[8,16,256]{2,1,0:T(8,128)S(1)}, f32[8,16,256]{2,1,0:T(8,128)}, u32[]{:S(2)}) copy-start(f32[8,16,256]{2,1,0:T(8,128)} %param.16) | copy-start | bytes 393220
  0.7 52.9 %copy-start.22 = (s32[16,256]{1,0:T(8,128)S(1)}, s32[16,256]{1,0:T(8,128)}, u32[]{:S(2)}) copy-start(s32[16,256]{1,0:T(8,128)} %param.20) | copy-start | bytes 49156
  0.7 50.6 %copy-start.47 = (s32[256]{0:T(256)S(1)}, s32[256]{0:T(256)}, u32[]{:S(2)}) copy-start(s32[256]{0:T(256)} %param.21) | copy-start | bytes 3076
  6.2 142.7 %collective-permute-start.3 = (f32[33,3,256]{2,0,1:T(8,128)}, f32[33,3,256]{2,0,1:T(8,128)}, u32[]{:S(2)}, u32[]{:S(2)}) collective-permute-start(f32[33,3,256]{2,0,1:T(8,128)} %get-tuple-element.96), channel_id=1, source_target_pairs={{1,0},{2,1},{3,2},{5,4},{6,5},{7,6},{9,8},{10,9},{11,10},{13,12},{... | collective-permute-start | bytes 304136 | tf_op jit(solution)/shard_map/ppermute | solution.py:25
  8.2 141.9 %collective-permute-start.2 = (f32[33,3,256]{2,0,1:T(8,128)}, f32[33,3,256]{2,0,1:T(8,128)}, u32[]{:S(2)}, u32[]{:S(2)}) collective-permute-start(f32[33,3,256]{2,0,1:T(8,128)} %get-tuple-element.95), channel_id=1, source_target_pairs={{0,1},{1,2},{2,3},{4,5},{5,6},{6,7},{8,9},{9,10},{10,11},{12,13},{... | collective-permute-start | bytes 304136 | tf_op jit(solution)/shard_map/ppermute | solution.py:23
  11.3 123.4 %collective-permute-start.1 = (f32[33,16,3]{2,1,0:T(8,128)S(1)}, f32[33,16,3]{2,1,0:T(8,128)S(1)}, u32[]{:S(2)}, u32[]{:S(2)}) collective-permute-start(f32[33,16,3]{2,1,0:T(8,128)S(1)} %get-tuple-element.104), channel_id=1, source_target_pairs={{4,0},{8,4},{12,8},{16,12},{20,16},{24,20},{28,24},{0,28},{5,1},{9... | collective-permute-start | bytes 19016 | tf_op jit(solution)/shard_map/ppermute | solution.py:25
  13.3 118.0 %collective-permute-start.9 = (f32[3,16,12]{2,1,0:T(8,128)}, f32[3,16,12]{2,1,0:T(8,128)S(1)}, u32[]{:S(2)}, u32[]{:S(2)}) collective-permute-start(f32[3,16,12]{2,1,0:T(8,128)} %get-tuple-element.153), channel_id=1, source_target_pairs={{4,0},{8,4},{12,8},{16,12},{20,16},{24,20},{28,24},{0,28},{5,1},{9... | collective-permute-start | bytes 6920 | tf_op jit(solution)/shard_map/ppermute | solution.py:25
  17.9 113.4 %collective-permute-start.8 = (f32[3,16,12]{2,1,0:T(8,128)}, f32[3,16,12]{2,1,0:T(8,128)}, u32[]{:S(2)}, u32[]{:S(2)}) collective-permute-start(f32[3,16,12]{2,1,0:T(8,128)} %get-tuple-element.152), channel_id=1, source_target_pairs={{0,4},{4,8},{8,12},{12,16},{16,20},{20,24},{24,28},{28,0},{1,5},{5... | collective-permute-start | bytes 6920 | tf_op jit(solution)/shard_map/ppermute | solution.py:23
  92.7 34.5 %copy-start.28 = (s32[1024]{0:T(1024)}, s32[1024]{0:T(1024)S(1)}, u32[]{:S(2)}) copy-start(s32[1024]{0:T(1024)S(1)} %pad_clamp_fusion) | copy-start | bytes 12292
  131.3 6.7 %collective-permute-start = (f32[33,16,3]{2,1,0:T(8,128)S(1)}, f32[33,16,3]{2,1,0:T(8,128)S(1)}, u32[]{:S(2)}, u32[]{:S(2)}) collective-permute-start(f32[33,16,3]{2,1,0:T(8,128)S(1)} %get-tuple-element.103), channel_id=1, source_target_pairs={{0,4},{4,8},{8,12},{12,16},{16,20},{20,24},{24,28},{28,0},{1,5},{5... | collective-permute-start | bytes 19016 | tf_op jit(solution)/shard_map/ppermute | solution.py:23
  132.8 87.1 %collective-permute-start.11 = (f32[3,12,280]{2,1,0:T(8,128)}, f32[3,12,280]{2,1,0:T(8,128)}, u32[]{:S(2)}, u32[]{:S(2)}) collective-permute-start(f32[3,12,280]{2,1,0:T(8,128)} %get-tuple-element.147), channel_id=1, source_target_pairs={{1,0},{2,1},{3,2},{5,4},{6,5},{7,6},{9,8},{10,9},{11,10},{13,12},{... | collective-permute-start | bytes 120968 | tf_op jit(solution)/shard_map/ppermute | solution.py:25
  134.8 86.1 %collective-permute-start.10 = (f32[3,12,280]{2,1,0:T(8,128)}, f32[3,12,280]{2,1,0:T(8,128)}, u32[]{:S(2)}, u32[]{:S(2)}) collective-permute-start(f32[3,12,280]{2,1,0:T(8,128)} %get-tuple-element.146), channel_id=1, source_target_pairs={{0,1},{1,2},{2,3},{4,5},{5,6},{6,7},{8,9},{9,10},{10,11},{12,13},{... | collective-permute-start | bytes 120968 | tf_op jit(solution)/shard_map/ppermute | solution.py:23
  163.4 58.6 %collective-permute-start.5 = (f32[3,16,12]{2,1,0:T(8,128)S(1)}, f32[3,16,12]{2,1,0:T(8,128)S(1)}, u32[]{:S(2)}, u32[]{:S(2)}) collective-permute-start(f32[3,16,12]{2,1,0:T(8,128)S(1)} %get-tuple-element.155), channel_id=1, source_target_pairs={{4,0},{8,4},{12,8},{16,12},{20,16},{24,20},{28,24},{0,28},{5,1},{9... | collective-permute-start | bytes 6920 | tf_op jit(solution)/shard_map/ppermute | solution.py:25
  166.9 55.1 %collective-permute-start.4 = (f32[3,16,12]{2,1,0:T(8,128)S(1)}, f32[3,16,12]{2,1,0:T(8,128)S(1)}, u32[]{:S(2)}, u32[]{:S(2)}) collective-permute-start(f32[3,16,12]{2,1,0:T(8,128)S(1)} %get-tuple-element.154), channel_id=1, source_target_pairs={{0,4},{4,8},{8,12},{12,16},{16,20},{20,24},{24,28},{28,0},{1,5},{5... | collective-permute-start | bytes 6920 | tf_op jit(solution)/shard_map/ppermute | solution.py:23
  203.3 18.7 %copy-start.19 = (f32[1,16,256]{2,1,0:T(8,128)S(1)}, f32[1,16,256]{2,1,0:T(8,128)}, u32[]{:S(2)}) copy-start(f32[1,16,256]{2,1,0:T(8,128)} %get-tuple-element.160) | copy-start | bytes 49156
  222.1 6.3 %collective-permute-start.7 = (f32[3,12,280]{2,1,0:T(8,128)S(1)}, f32[3,12,280]{2,1,0:T(8,128)S(1)}, u32[]{:S(2)}, u32[]{:S(2)}) collective-permute-start(f32[3,12,280]{2,1,0:T(8,128)S(1)} %get-tuple-element.149), channel_id=1, source_target_pairs={{1,0},{2,1},{3,2},{5,4},{6,5},{7,6},{9,8},{10,9},{11,10},{13,12},{... | collective-permute-start | bytes 120968 | tf_op jit(solution)/shard_map/ppermute | solution.py:25
  224.1 5.7 %collective-permute-start.6 = (f32[3,12,280]{2,1,0:T(8,128)S(1)}, f32[3,12,280]{2,1,0:T(8,128)S(1)}, u32[]{:S(2)}, u32[]{:S(2)}) collective-permute-start(f32[3,12,280]{2,1,0:T(8,128)S(1)} %get-tuple-element.148), channel_id=1, source_target_pairs={{0,1},{1,2},{2,3},{4,5},{5,6},{6,7},{8,9},{9,10},{10,11},{12,13},{... | collective-permute-start | bytes 120968 | tf_op jit(solution)/shard_map/ppermute | solution.py:23
  232.1 54.1 %collective-permute-start.13 = (f32[3,16,12]{2,1,0:T(8,128)S(1)}, f32[3,16,12]{2,1,0:T(8,128)S(1)}, u32[]{:S(2)}, u32[]{:S(2)}) collective-permute-start(f32[3,16,12]{2,1,0:T(8,128)S(1)} %get-tuple-element.151), channel_id=1, source_target_pairs={{4,0},{8,4},{12,8},{16,12},{20,16},{24,20},{28,24},{0,28},{5,1},{9... | collective-permute-start | bytes 6920 | tf_op jit(solution)/shard_map/ppermute | solution.py:25
  232.2 54.0 %collective-permute-start.12 = (f32[3,16,12]{2,1,0:T(8,128)S(1)}, f32[3,16,12]{2,1,0:T(8,128)S(1)}, u32[]{:S(2)}, u32[]{:S(2)}) collective-permute-start(f32[3,16,12]{2,1,0:T(8,128)S(1)} %get-tuple-element.150), channel_id=1, source_target_pairs={{0,4},{4,8},{8,12},{12,16},{16,20},{20,24},{24,28},{28,0},{1,5},{5... | collective-permute-start | bytes 6920 | tf_op jit(solution)/shard_map/ppermute | solution.py:23
  286.3 5.6 %collective-permute-start.15 = (f32[3,12,280]{2,1,0:T(8,128)S(1)}, f32[3,12,280]{2,1,0:T(8,128)S(1)}, u32[]{:S(2)}, u32[]{:S(2)}) collective-permute-start(f32[3,12,280]{2,1,0:T(8,128)S(1)} %get-tuple-element.145), channel_id=1, source_target_pairs={{1,0},{2,1},{3,2},{5,4},{6,5},{7,6},{9,8},{10,9},{11,10},{13,12},{... | collective-permute-start | bytes 120968 | tf_op jit(solution)/shard_map/ppermute | solution.py:25
  288.3 5.7 %collective-permute-start.14 = (f32[3,12,280]{2,1,0:T(8,128)S(1)}, f32[3,12,280]{2,1,0:T(8,128)S(1)}, u32[]{:S(2)}, u32[]{:S(2)}) collective-permute-start(f32[3,12,280]{2,1,0:T(8,128)S(1)} %get-tuple-element.144), channel_id=1, source_target_pairs={{0,1},{1,2},{2,3},{4,5},{5,6},{6,7},{8,9},{9,10},{10,11},{12,13},{... | collective-permute-start | bytes 120968 | tf_op jit(solution)/shard_map/ppermute | solution.py:23
  (40 other events, 402.1 us)
